TPU v7x, 32 devices: a whole 2x2x4 slice. The times are simulated.
32 devices in a mesh: plant: 8 (over z, core), col: 4 (over y, x).
Axes of the slice: x: 2, y: 2, z: 4, core: 2. Of those that a mesh axis runs over, the one named last changes fastest.
Arguments:
- tiles: bfloat16 [8, 4, 48, 256, 256], P('plant', 'col'), may hold values from -0.109375 to 0.109375
- tile_row: int32 [8, 4, 48], P('plant', 'col'), may hold values from 0 to 15
- tile_col: int32 [8, 4, 48], P('plant', 'col'), may hold values from 0 to 63
- row_count: int32 [8], P('plant'), may hold values from 2048 to 4096, as said below
- x_start: float32 [32, 65536], P(None, 'col'), may hold values from 0 to 1
- y_start: float32 [32, 32768], P(None, 'plant'), may hold values from 0 to 1
- cost: float32 [65536], P('col'), may hold values from -3 to 3
- upper: float32 [65536], P('col'), may hold values from 0.5 to 2
- demand: float32 [32, 32768], P(None, 'plant'), may hold values from -6 to 6
- tau: float32 [32], replicated, may hold values from 0.2 to 1
- sigma: float32 [32], replicated, may hold values from 0.2 to 1
Outputs:
- primal: float32 [32, 65536], P(None, 'col')
- dual: float32 [32, 32768], P(None, 'plant')
Inputs may be any that keep to these rules, and one draw needn't show every extreme that they name: Each plant block has row_count live rows, the first ones of its block; at least one plant block is full. `tile_row`: tiles at the same position add up.
All inputs are finite; a program needn't handle non-finite values.
Results may differ from a plain program's by a relative error of at most 0.003.
Values sent between devices are 32-bit elements; how exact they have to be, the bound alone decides.
No kernel may reach another device: no remote copies, remote signals or barrier semaphores. Data moves between devices by JAX's collectives and lax.ppermute only.
A program may use at most 64 MiB of HBM per device.

v0:
```python
import jax
import jax.numpy as jnp
from jax import lax
from jax.sharding import PartitionSpec as P

ITERS = 3


def body(tiles, tile_row, tile_col, row_count, x_start, y_start, cost, upper, demand, tau, sigma):
    blocks = tiles[0, 0]
    rows = tile_row[0, 0]
    cols = tile_col[0, 0]
    tile_width = blocks.shape[1]
    scenarios, rows_dev = y_start.shape
    col_width = x_start.shape[1]
    row_tiles = rows_dev // tile_width
    col_tiles = col_width // tile_width
    live = (jnp.arange(rows_dev, dtype=jnp.int32) < row_count[0]).astype(jnp.float32)[None, :]
    row_hot = (jnp.arange(row_tiles, dtype=jnp.int32)[:, None] == rows[None, :]).astype(jnp.float32)
    col_hot = (jnp.arange(col_tiles, dtype=jnp.int32)[:, None] == cols[None, :]).astype(jnp.float32)
    step_primal = tau[:, None]
    step_dual = sigma[:, None]
    cost_row = cost[None, :]
    upper_row = upper[None, :]
    primal = x_start
    dual = y_start * live
    for iteration in range(ITERS):
        dual_low = dual.astype(jnp.bfloat16).reshape(scenarios, row_tiles, tile_width)
        picked = jnp.take(dual_low, rows, axis=1)
        contrib = jnp.einsum("str,trc->stc", picked, blocks, preferred_element_type=jnp.float32)
        kty_part = jnp.einsum(
            "kt,stc->skc", col_hot, contrib, precision=lax.Precision.HIGHEST
        ).reshape(scenarios, col_width)
        kty = lax.psum(kty_part, "plant")
        primal_new = jnp.minimum(
            jnp.maximum(primal - step_primal * (cost_row - kty), 0.0), upper_row
        )
        extra = (
            (2.0 * primal_new - primal)
            .astype(jnp.bfloat16)
            .reshape(scenarios, col_tiles, tile_width)
        )
        chosen = jnp.take(extra, cols, axis=1)
        product = jnp.einsum("stc,trc->str", chosen, blocks, preferred_element_type=jnp.float32)
        kx_part = jnp.einsum(
            "kt,str->skr", row_hot, product, precision=lax.Precision.HIGHEST
        ).reshape(scenarios, rows_dev)
        kx = lax.psum(kx_part, "col")
        dual = jnp.maximum(dual + step_dual * (demand - kx), 0.0) * live
        primal = primal_new
    return (primal, dual)


def solution(mesh):
    placed = (
        P("plant", "col", None, None, None),
        P("plant", "col", None),
        P("plant", "col", None),
        P("plant"),
        P(None, "col"),
        P(None, "plant"),
        P("col"),
        P("col"),
        P(None, "plant"),
        P(),
        P(),
    )
    return jax.shard_map(
        body,
        mesh=mesh,
        in_specs=placed,
        out_specs=(P(None, "col"), P(None, "plant")),
        check_vma=False,
    )
```

profile of v0, /device:TPU:0, one launch (start us, length us, event | category | flops | bytes accessed | tf_op | source)
XLA Modules:
  0.0 428.5 jit_solution(13103330824339237959)
XLA Ops:
  11.0 4.0 fusion.24
  15.0 2.1 fusion.22
  17.1 2.5 copy.31
  19.8 67.6 %all-reduce.7.cloned.1.call-done = f32[32,16384]{1,0:T(8,128)} async-done(((f32[32,16384]{1,0:T(8,128)}), f32[32,16384]{1,0:T(8,128)}) %all-reduce.7.cloned.1.call-update) | async-done | bytes 2097168 | tf_op jit(solution)/shard_map/psum | solution.py:34
  87.4 2.2 subtract_convert_fusion.2
  90.7 1.8 gather_fusion.1
  92.6 4.7 %fusion.27 = f32[32,48,256]{2,0,1:T(8,128)S(1)} fusion(bf16[1,1,48,256,256]{4,3,2,1,0:T(8,128)(2,1)} %param.15, bf16[48,32,256]{2,1,0:T(8,128)(2,1)S(1)} %gather_fusion.1, pred[48]{0:T(512)(128)(4,1)S(1)} %compare_and_fusion), kind=kOutput, calls=%fused_computation.37 | convolution fusion | flops 201719808 | bytes 8650800 | tf_op jit(solution)/shard_map/stc,trc->str/dot_general | solution.py:44
  100.2 44.9 %all-reduce.9.cloned.1.call-done = f32[32,4096]{1,0:T(8,128)} async-done(((f32[32,4096]{1,0:T(8,128)}), f32[32,4096]{1,0:T(8,128)}) %all-reduce.9.cloned.1.call-update) | async-done | bytes 524304 | tf_op jit(solution)/shard_map/psum | solution.py:48
  148.1 4.3 fusion.30
  152.4 2.2 fusion.18
  154.5 2.5 copy.33
  157.1 65.0 %all-reduce.11.cloned.1.call-done = f32[32,16384]{1,0:T(8,128)} async-done(((f32[32,16384]{1,0:T(8,128)}), f32[32,16384]{1,0:T(8,128)}) %all-reduce.11.cloned.1.call-update) | async-done | bytes 2097168 | tf_op jit(solution)/shard_map/psum | solution.py:34
  222.1 3.1 subtract_convert_fusion.1
  226.4 2.9 gather_fusion.3
  229.3 5.0 %fusion.33 = f32[32,48,256]{2,0,1:T(8,128)S(1)} fusion(bf16[1,1,48,256,256]{4,3,2,1,0:T(8,128)(2,1)} %param.15, bf16[48,32,256]{2,1,0:T(8,128)(2,1)} %gather_fusion.3, pred[48]{0:T(512)(128)(4,1)S(1)} %copy-done.12), kind=kOutput, calls=%fused_computation.39 | convolution fusion | flops 201719808 | bytes 8650800 | tf_op jit(solution)/shard_map/stc,trc->str/dot_general | solution.py:44
  237.2 44.9 %all-reduce.13.cloned.1.call-done = f32[32,4096]{1,0:T(8,128)} async-done(((f32[32,4096]{1,0:T(8,128)}), f32[32,4096]{1,0:T(8,128)}) %all-reduce.13.cloned.1.call-update) | async-done | bytes 524304 | tf_op jit(solution)/shard_map/psum | solution.py:48
  285.2 4.3 fusion.36
  289.5 2.1 fusion.14
  291.6 2.5 copy.35
  294.3 65.0 %all-reduce.15.cloned.1.call-done = f32[32,16384]{1,0:T(8,128)} async-done(((f32[32,16384]{1,0:T(8,128)}), f32[32,16384]{1,0:T(8,128)}) %all-reduce.15.cloned.1.call-update) | async-done | bytes 2097168 | tf_op jit(solution)/shard_map/psum | solution.py:34
  359.3 5.4 %subtract_convert_fusion = (bf16[32,16384]{1,0:T(8,128)(2,1)S(1)}, f32[32,16384]{1,0:T(8,128)}) fusion(f32[32,16384]{1,0:T(8,128)} %all-reduce.11.cloned.1.call-done, f32[16384]{0:T(1024)S(1)} %copy-done.4, f32[32,16384]{1,0:T(8,128)S(1)} %copy-done, f32[32,16384]{1,0:T(8,128)} %all-reduce.7.cloned.1.call-done, f32[16384]{0:T(1024)S(1)} %copy-done.5, ...), kind=kLoop, calls=%fused_computation.18 | loop fusion | flops 9437184 | bytes 11665536 | tf_op jit(solution)/shard_map/convert_element_type | solution.py:40
  366.5 5.0 %fusion.39 = f32[32,48,256]{2,0,1:T(8,128)S(1)} fusion(bf16[1,1,48,256,256]{4,3,2,1,0:T(8,128)(2,1)} %param.15, bf16[48,32,256]{2,1,0:T(8,128)(2,1)} %gather_fusion.5, pred[48]{0:T(512)(128)(4,1)S(1)} %copy-done.13), kind=kOutput, calls=%fused_computation.41 | convolution fusion | flops 201719808 | bytes 8650800 | tf_op jit(solution)/shard_map/stc,trc->str/dot_general | solution.py:44
  374.2 45.1 %all-reduce.17.cloned.1.call-done = f32[32,4096]{1,0:T(8,128)} async-done(((f32[32,4096]{1,0:T(8,128)}), f32[32,4096]{1,0:T(8,128)}) %all-reduce.17.cloned.1.call-update) | async-done | bytes 524304 | tf_op jit(solution)/shard_map/psum | solution.py:48
  419.3 2.3 maximum_multiply_fusion
  (86 shorter events, 21.8 us)
Async XLA Ops:
  7.2 80.3 %all-reduce.7.cloned.1.call-start = ((), (), s32[]{:S(2)}) async-start(), calls=%async_computation | async-start | bytes 4194304 | tf_op jit(solution)/shard_map/psum | solution.py:34
  7.9 7.1 %copy-start.14 = (pred[48]{0:T(512)(128)(4,1)}, pred[48]{0:T(512)(128)(4,1)S(1)}, u32[]{:S(2)}) copy-start(pred[48]{0:T(512)(128)(4,1)S(1)} %compare_and_fusion.1) | copy-start | bytes 148
  9.2 5.8 %copy-start.7 = (s32[1024]{0:T(1024)}, s32[1024]{0:T(1024)S(1)}, u32[]{:S(2)}) copy-start(s32[1024]{0:T(1024)S(1)} %pad_clamp_fusion.1) | copy-start | bytes 12292
  17.1 70.3 %copy-start.4 = (f32[16384]{0:T(1024)S(1)}, f32[16384]{0:T(1024)}, u32[]{:S(2)}) copy-start(f32[16384]{0:T(1024)} %param.22) | copy-start | bytes 196612
  17.1 70.3 %copy-start.5 = (f32[16384]{0:T(1024)S(1)}, f32[16384]{0:T(1024)}, u32[]{:S(2)}) copy-start(f32[16384]{0:T(1024)} %param.21) | copy-start | bytes 196612
  19.7 67.8 %copy-start = (f32[32,16384]{1,0:T(8,128)S(1)}, f32[32,16384]{1,0:T(8,128)}, u32[]{:S(2)}) copy-start(f32[32,16384]{1,0:T(8,128)} %param.19) | copy-start | bytes 6291460
  19.7 67.8 %copy-start.18 = (f32[32]{0:T(128)S(1)}, f32[32]{0:T(128)}, u32[]{:S(2)}) copy-start(f32[32]{0:T(128)} %param.24) | copy-start | bytes 388
  19.7 125.4 %all-reduce.9.cloned.1.call-start = ((), (), s32[]{:S(2)}) async-start(), calls=%async_computation.1 | async-start | bytes 1048576 | tf_op jit(solution)/shard_map/psum | solution.py:48
  19.8 70.9 %copy-start.6 = (s32[1024]{0:T(1024)}, s32[1024]{0:T(1024)S(1)}, u32[]{:S(2)}) copy-start(s32[1024]{0:T(1024)S(1)} %pad_clamp_fusion) | copy-start | bytes 12292
  19.8 72.8 %copy-start.11 = (pred[48]{0:T(512)(128)(4,1)}, pred[48]{0:T(512)(128)(4,1)S(1)}, u32[]{:S(2)}) copy-start(pred[48]{0:T(512)(128)(4,1)S(1)} %compare_and_fusion) | copy-start | bytes 148
  97.3 47.8 %copy-start.1 = (f32[32,4096]{1,0:T(8,128)S(1)}, f32[32,4096]{1,0:T(8,128)}, u32[]{:S(2)}) copy-start(f32[32,4096]{1,0:T(8,128)} %param.20) | copy-start | bytes 1572868
  97.3 47.8 %copy-start.2 = (f32[32,4096]{1,0:T(8,128)S(1)}, f32[32,4096]{1,0:T(8,128)}, u32[]{:S(2)}) copy-start(f32[32,4096]{1,0:T(8,128)} %param.23) | copy-start | bytes 1572868
  97.3 47.8 %copy-start.15 = (f32[32]{0:T(128)S(1)}, f32[32]{0:T(128)}, u32[]{:S(2)}) copy-start(f32[32]{0:T(128)} %param.25) | copy-start | bytes 388
  100.0 122.1 %all-reduce.11.cloned.1.call-start = ((), (), s32[]{:S(2)}) async-start(), calls=%async_computation.2 | async-start | bytes 4194304 | tf_op jit(solution)/shard_map/psum | solution.py:34
  157.0 65.1 %copy-start.19 = (f32[32]{0:T(128)S(1)}, f32[32]{0:T(128)}, u32[]{:S(2)}) copy-start(f32[32]{0:T(128)} %param.24) | copy-start | bytes 388
  157.1 125.0 %all-reduce.13.cloned.1.call-start = ((), (), s32[]{:S(2)}) async-start(), calls=%async_computation.3 | async-start | bytes 1048576 | tf_op jit(solution)/shard_map/psum | solution.py:48
  229.3 5.0 %copy-start.9 = (s32[1,1,48]{2,1,0:T(1,128)S(1)}, s32[1,1,48]{2,1,0:T(1,128)}, u32[]{:S(2)}) copy-start(s32[1,1,48]{2,1,0:T(1,128)} %param.16) | copy-start | bytes 580
  234.3 47.8 %copy-start.16 = (f32[32]{0:T(128)S(1)}, f32[32]{0:T(128)}, u32[]{:S(2)}) copy-start(f32[32]{0:T(128)} %param.25) | copy-start | bytes 388
  236.9 122.3 %all-reduce.15.cloned.1.call-start = ((), (), s32[]{:S(2)}) async-start(), calls=%async_computation.4 | async-start | bytes 4194304 | tf_op jit(solution)/shard_map/psum | solution.py:34
  294.2 65.1 %copy-start.20 = (f32[32]{0:T(128)S(1)}, f32[32]{0:T(128)}, u32[]{:S(2)}) copy-start(f32[32]{0:T(128)} %param.24) | copy-start | bytes 388
  294.2 125.1 %all-reduce.17.cloned.1.call-start = ((), (), s32[]{:S(2)}) async-start(), calls=%async_computation.5 | async-start | bytes 1048576 | tf_op jit(solution)/shard_map/psum | solution.py:48
  366.5 5.0 %copy-start.10 = (s32[1,1,48]{2,1,0:T(1,128)S(1)}, s32[1,1,48]{2,1,0:T(1,128)}, u32[]{:S(2)}) copy-start(s32[1,1,48]{2,1,0:T(1,128)} %param.16) | copy-start | bytes 580
  371.5 47.8 %copy-start.3 = (f32[32,4096]{1,0:T(8,128)S(1)}, f32[32,4096]{1,0:T(8,128)}, u32[]{:S(2)}) copy-start(f32[32,4096]{1,0:T(8,128)} %all-reduce.9.cloned.1.call-done) | copy-start | bytes 1572868
  371.5 47.8 %copy-start.17 = (f32[32]{0:T(128)S(1)}, f32[32]{0:T(128)}, u32[]{:S(2)}) copy-start(f32[32]{0:T(128)} %param.25) | copy-start | bytes 388
  (6 other events, 23.1 us)
Sparse Core Ops, SparseCore 0:
  19.8 67.5 all-reduce.6
  100.1 44.9 all-reduce.8
  157.2 64.8 all-reduce.10
  237.1 44.9 all-reduce.12
  294.3 64.8 all-reduce.14
  374.3 44.9 all-reduce.16
where the time goes:
time: 429 us; the launch traced here: 428 us
  waiting for transfers between devices  333 us (78%)
  matrix products  38.2 us (9%)
  local copies, waits for them, and re-layouts  23.7 us (6%)
  other arithmetic  18.2 us (4%)
  between operations  15.1 us (4%)
    psum x3, waiting for transfers between devices, body(): kty = lax.psum(kty_part, 'plant')  198 us
    psum x3, waiting for transfers between devices, body(): kx = lax.psum(kx_part, 'col')  135 us
    dot_general x3, matrix products, body(): jnp.einsum('stc,trc->str', chosen, blocks, preferred_element_type=jnp.flo...  14.7 us
    dot_general x3, matrix products, body(): jnp.einsum('str,trc->stc', picked, blocks, preferred_element_type=jnp.flo...  12.5 us
    unnamed x54, local copies, waits for them, and re-layouts  11 us
    convert_element_type x3, other arithmetic, body(): extra = (2.0 * primal_new - primal).astype(jnp.bfloat16).reshape(scenario...  10.7 us
  transfers between devices with their start and end apart: 6, of which 6 were waited for; matrix products, arithmetic and copies ran while one was open for 0% of the time, Pallas kernels for 0%

commit v1 on v0

--- a/solution.py
+++ b/solution.py
@@ -45,7 +45,8 @@
         kx_part = jnp.einsum(
             "kt,str->skr", row_hot, product, precision=lax.Precision.HIGHEST
         ).reshape(scenarios, rows_dev)
-        kx = lax.psum(kx_part, "col")
+        terms = lax.all_gather(kx_part, "col", axis=0, tiled=False)
+        kx = terms.sum(axis=0)
         dual = jnp.maximum(dual + step_dual * (demand - kx), 0.0) * live
         primal = primal_new
     return (primal, dual)

time: 429 us -> 405 us (0.944)
  waiting for transfers between devices: 333 us -> 303 us
  other arithmetic: 18.2 us -> 23 us
    psum x3 -> x0, waiting for transfers between devices: 135 us -> none  [body(): kx = lax.psum(kx_part, 'col')]
    all_gather x0 -> x3, waiting for transfers between devices: none -> 105 us  [body(): terms = lax.all_gather(kx_part, 'col', axis=0, tiled=False)]
    reduce_sum x0 -> x3, other arithmetic: none -> 6.06 us  [body(): kx = terms.sum(axis=0)]
    unnamed x54 -> x51, local copies, waits for them, and re-layouts: 11 us -> 7.72 us
where the time goes in v1:
time: 405 us; the launch traced here: 404 us
  waiting for transfers between devices  303 us (75%)
  matrix products  38.9 us (10%)
  local copies, waits for them, and re-layouts  24.1 us (6%)
  other arithmetic  23 us (6%)
  between operations  15.2 us (4%)
    psum x3, waiting for transfers between devices, body(): kty = lax.psum(kty_part, 'plant')  198 us
    all_gather x3, waiting for transfers between devices, body(): terms = lax.all_gather(kx_part, 'col', axis=0, tiled=False)  105 us
    dot_general x3, matrix products, body(): jnp.einsum('stc,trc->str', chosen, blocks, preferred_element_type=jnp.flo...  14.7 us
    dot_general x3, matrix products, body(): jnp.einsum('str,trc->stc', picked, blocks, preferred_element_type=jnp.flo...  12.5 us
    convert_element_type x3, other arithmetic, body(): extra = (2.0 * primal_new - primal).astype(jnp.bfloat16).reshape(scenario...  10.7 us
  transfers between devices with their start and end apart: 6, of which 6 were waited for; matrix products, arithmetic and copies ran while one was open for 0% of the time, Pallas kernels for 0%

profile of v1, /device:TPU:0, one launch (start us, length us, event | category | flops | bytes accessed | tf_op | source)
XLA Modules:
  0.0 404.5 jit_solution(8562749732752084734)
XLA Ops:
  11.0 4.0 fusion.24
  15.0 2.1 fusion.22
  17.1 2.5 copy.43
  19.8 67.6 %all-reduce.4.cloned.1.call-done = f32[32,16384]{1,0:T(8,128)} async-done(((f32[32,16384]{1,0:T(8,128)}), f32[32,16384]{1,0:T(8,128)}) %all-reduce.4.cloned.1.call-update) | async-done | bytes 2097168 | tf_op jit(solution)/shard_map/psum | solution.py:34
  87.4 2.2 subtract_convert_fusion.2
  92.6 4.7 %fusion.27 = f32[32,48,256]{2,0,1:T(8,128)S(1)} fusion(bf16[1,1,48,256,256]{4,3,2,1,0:T(8,128)(2,1)} %param.15, bf16[48,32,256]{2,1,0:T(8,128)(2,1)S(1)} %gather_fusion.1, pred[48]{0:T(512)(128)(4,1)S(1)} %compare_and_fusion), kind=kOutput, calls=%fused_computation.37 | convolution fusion | flops 201719808 | bytes 8650800 | tf_op jit(solution)/shard_map/stc,trc->str/dot_general | solution.py:44
  100.0 34.9 %all-gather.4.cloned.1.call-done = f32[4,32,4096]{2,1,0:T(8,128)} async-done(((f32[1,32,4096]{2,1,0:T(8,128)}), f32[4,32,4096]{2,1,0:T(8,128)}) %all-gather.4.cloned.1.call-update) | async-done | bytes 2097168 | tf_op jit(solution)/shard_map/all_gather | solution.py:48
  139.6 4.3 %fusion.30 = f32[32,48,256]{2,0,1:T(8,128)S(1)} fusion(bf16[1,1,48,256,256]{4,3,2,1,0:T(8,128)(2,1)} %param.15, bf16[48,32,256]{2,1,0:T(8,128)(2,1)} %gather_fusion.2, pred[48]{0:T(512)(128)(4,1)} %copy-done.14), kind=kOutput, calls=%fused_computation.38 | convolution fusion | flops 201719808 | bytes 8650800 | tf_op jit(solution)/shard_map/str,trc->stc/dot_general | solution.py:30
  143.9 2.1 fusion.18
  146.0 2.5 copy.44
  148.6 65.0 %all-reduce.6.cloned.1.call-done = f32[32,16384]{1,0:T(8,128)} async-done(((f32[32,16384]{1,0:T(8,128)}), f32[32,16384]{1,0:T(8,128)}) %all-reduce.6.cloned.1.call-update) | async-done | bytes 2097168 | tf_op jit(solution)/shard_map/psum | solution.py:34
  213.6 3.1 subtract_convert_fusion.1
  217.9 2.9 gather_fusion.3
  220.7 5.0 %fusion.33 = f32[32,48,256]{2,0,1:T(8,128)S(1)} fusion(bf16[1,1,48,256,256]{4,3,2,1,0:T(8,128)(2,1)} %param.15, bf16[48,32,256]{2,1,0:T(8,128)(2,1)} %gather_fusion.3, pred[48]{0:T(512)(128)(4,1)S(1)} %copy-done.12), kind=kOutput, calls=%fused_computation.39 | convolution fusion | flops 201719808 | bytes 8650800 | tf_op jit(solution)/shard_map/stc,trc->str/dot_general | solution.py:44
  225.7 2.3 fusion.45
  230.3 34.8 %all-gather.6.cloned.1.call-done = f32[4,32,4096]{2,1,0:T(8,128)} async-done(((f32[1,32,4096]{2,1,0:T(8,128)}), f32[4,32,4096]{2,1,0:T(8,128)}) %all-gather.6.cloned.1.call-update) | async-done | bytes 2097168 | tf_op jit(solution)/shard_map/all_gather | solution.py:48
  265.1 2.5 reduce_sum.28
  270.8 4.3 %fusion.36 = f32[32,48,256]{2,0,1:T(8,128)S(1)} fusion(bf16[1,1,48,256,256]{4,3,2,1,0:T(8,128)(2,1)} %param.15, bf16[48,32,256]{2,1,0:T(8,128)(2,1)} %gather_fusion.4, pred[48]{0:T(512)(128)(4,1)} %copy-done.14), kind=kOutput, calls=%fused_computation.40 | convolution fusion | flops 201719808 | bytes 8650800 | tf_op jit(solution)/shard_map/str,trc->stc/dot_general | solution.py:30
  275.1 2.1 fusion.14
  277.2 2.5 copy.45
  279.9 65.0 %all-reduce.8.cloned.1.call-done = f32[32,16384]{1,0:T(8,128)} async-done(((f32[32,16384]{1,0:T(8,128)}), f32[32,16384]{1,0:T(8,128)}) %all-reduce.8.cloned.1.call-update) | async-done | bytes 2097168 | tf_op jit(solution)/shard_map/psum | solution.py:34
  344.9 5.4 %subtract_convert_fusion = (bf16[32,16384]{1,0:T(8,128)(2,1)S(1)}, f32[32,16384]{1,0:T(8,128)}) fusion(f32[32,16384]{1,0:T(8,128)} %all-reduce.6.cloned.1.call-done, f32[16384]{0:T(1024)S(1)} %copy-done.4, f32[32,16384]{1,0:T(8,128)S(1)} %copy-done, f32[32,16384]{1,0:T(8,128)} %all-reduce.4.cloned.1.call-done, f32[16384]{0:T(1024)S(1)} %copy-done.5, ...), kind=kLoop, calls=%fused_computation.18 | loop fusion | flops 9437184 | bytes 11665536 | tf_op jit(solution)/shard_map/convert_element_type | solution.py:40
  352.1 5.0 %fusion.39 = f32[32,48,256]{2,0,1:T(8,128)S(1)} fusion(bf16[1,1,48,256,256]{4,3,2,1,0:T(8,128)(2,1)} %param.15, bf16[48,32,256]{2,1,0:T(8,128)(2,1)} %gather_fusion.5, pred[48]{0:T(512)(128)(4,1)S(1)} %copy-done.13), kind=kOutput, calls=%fused_computation.41 | convolution fusion | flops 201719808 | bytes 8650800 | tf_op jit(solution)/shard_map/stc,trc->str/dot_general | solution.py:44
  359.6 35.1 %all-gather.8.cloned.1.call-done = f32[4,32,4096]{2,1,0:T(8,128)} async-done(((f32[1,32,4096]{2,1,0:T(8,128)}), f32[4,32,4096]{2,1,0:T(8,128)}) %all-gather.8.cloned.1.call-update) | async-done | bytes 2097168 | tf_op jit(solution)/shard_map/all_gather | solution.py:48
  (89 shorter events, 27.2 us)
Async XLA Ops:
  7.2 80.3 %all-reduce.4.cloned.1.call-start = ((), (), s32[]{:S(2)}) async-start(), calls=%async_computation | async-start | bytes 4194304 | tf_op jit(solution)/shard_map/psum | solution.py:34
  7.9 7.1 %copy-start.14 = (pred[48]{0:T(512)(128)(4,1)}, pred[48]{0:T(512)(128)(4,1)S(1)}, u32[]{:S(2)}) copy-start(pred[48]{0:T(512)(128)(4,1)S(1)} %compare_and_fusion.1) | copy-start | bytes 148
  9.2 5.8 %copy-start.7 = (s32[1024]{0:T(1024)}, s32[1024]{0:T(1024)S(1)}, u32[]{:S(2)}) copy-start(s32[1024]{0:T(1024)S(1)} %pad_clamp_fusion.1) | copy-start | bytes 12292
  17.1 70.3 %copy-start.4 = (f32[16384]{0:T(1024)S(1)}, f32[16384]{0:T(1024)}, u32[]{:S(2)}) copy-start(f32[16384]{0:T(1024)} %param.22) | copy-start | bytes 196612
  17.1 70.3 %copy-start.5 = (f32[16384]{0:T(1024)S(1)}, f32[16384]{0:T(1024)}, u32[]{:S(2)}) copy-start(f32[16384]{0:T(1024)} %param.21) | copy-start | bytes 196612
  19.7 67.8 %copy-start = (f32[32,16384]{1,0:T(8,128)S(1)}, f32[32,16384]{1,0:T(8,128)}, u32[]{:S(2)}) copy-start(f32[32,16384]{1,0:T(8,128)} %param.19) | copy-start | bytes 6291460
  19.7 67.8 %copy-start.18 = (f32[32]{0:T(128)S(1)}, f32[32]{0:T(128)}, u32[]{:S(2)}) copy-start(f32[32]{0:T(128)} %param.24) | copy-start | bytes 388
  19.7 115.2 %all-gather.4.cloned.1.call-start = ((), (), s32[]{:S(2)}) async-start(), calls=%async_computation.1 | async-start | bytes 2621440 | tf_op jit(solution)/shard_map/all_gather | solution.py:48
  19.8 70.9 %copy-start.6 = (s32[1024]{0:T(1024)}, s32[1024]{0:T(1024)S(1)}, u32[]{:S(2)}) copy-start(s32[1024]{0:T(1024)S(1)} %pad_clamp_fusion) | copy-start | bytes 12292
  19.8 72.8 %copy-start.11 = (pred[48]{0:T(512)(128)(4,1)}, pred[48]{0:T(512)(128)(4,1)S(1)}, u32[]{:S(2)}) copy-start(pred[48]{0:T(512)(128)(4,1)S(1)} %compare_and_fusion) | copy-start | bytes 148
  98.9 37.8 %copy-start.1 = (f32[32,4096]{1,0:T(8,128)S(1)}, f32[32,4096]{1,0:T(8,128)}, u32[]{:S(2)}) copy-start(f32[32,4096]{1,0:T(8,128)} %param.20) | copy-start | bytes 1572868
  98.9 37.8 %copy-start.15 = (f32[32]{0:T(128)S(1)}, f32[32]{0:T(128)}, u32[]{:S(2)}) copy-start(f32[32]{0:T(128)} %param.25) | copy-start | bytes 388
  99.8 113.8 %all-reduce.6.cloned.1.call-start = ((), (), s32[]{:S(2)}) async-start(), calls=%async_computation.2 | async-start | bytes 4194304 | tf_op jit(solution)/shard_map/psum | solution.py:34
  148.6 65.0 %copy-start.19 = (f32[32]{0:T(128)S(1)}, f32[32]{0:T(128)}, u32[]{:S(2)}) copy-start(f32[32]{0:T(128)} %param.24) | copy-start | bytes 388
  148.6 116.5 %all-gather.6.cloned.1.call-start = ((), (), s32[]{:S(2)}) async-start(), calls=%async_computation.3 | async-start | bytes 2621440 | tf_op jit(solution)/shard_map/all_gather | solution.py:48
  220.7 5.0 %copy-start.9 = (s32[1,1,48]{2,1,0:T(1,128)S(1)}, s32[1,1,48]{2,1,0:T(1,128)}, u32[]{:S(2)}) copy-start(s32[1,1,48]{2,1,0:T(1,128)} %param.16) | copy-start | bytes 580
  228.1 39.6 %copy-start.16 = (f32[32]{0:T(128)S(1)}, f32[32]{0:T(128)}, u32[]{:S(2)}) copy-start(f32[32]{0:T(128)} %param.25) | copy-start | bytes 388
  230.0 114.9 %all-reduce.8.cloned.1.call-start = ((), (), s32[]{:S(2)}) async-start(), calls=%async_computation.4 | async-start | bytes 4194304 | tf_op jit(solution)/shard_map/psum | solution.py:34
  279.8 65.1 %copy-start.20 = (f32[32]{0:T(128)S(1)}, f32[32]{0:T(128)}, u32[]{:S(2)}) copy-start(f32[32]{0:T(128)} %param.24) | copy-start | bytes 388
  279.8 114.9 %all-gather.8.cloned.1.call-start = ((), (), s32[]{:S(2)}) async-start(), calls=%async_computation.5 | async-start | bytes 2621440 | tf_op jit(solution)/shard_map/all_gather | solution.py:48
  352.1 5.0 %copy-start.10 = (s32[1,1,48]{2,1,0:T(1,128)S(1)}, s32[1,1,48]{2,1,0:T(1,128)}, u32[]{:S(2)}) copy-start(s32[1,1,48]{2,1,0:T(1,128)} %param.16) | copy-start | bytes 580
  358.7 37.8 %copy-start.2 = (f32[32,4096]{1,0:T(8,128)S(1)}, f32[32,4096]{1,0:T(8,128)}, u32[]{:S(2)}) copy-start(f32[32,4096]{1,0:T(8,128)} %param.23) | copy-start | bytes 1572868
  358.7 37.8 %copy-start.3 = (f32[32,4096]{1,0:T(8,128)S(1)}, f32[32,4096]{1,0:T(8,128)}, u32[]{:S(2)}) copy-start(f32[32,4096]{1,0:T(8,128)} %reduce_sum.28) | copy-start | bytes 1572868
  358.7 37.8 %copy-start.17 = (f32[32]{0:T(128)S(1)}, f32[32]{0:T(128)}, u32[]{:S(2)}) copy-start(f32[32]{0:T(128)} %param.25) | copy-start | bytes 388
  (6 other events, 23.1 us)
Sparse Core Ops, SparseCore 0:
  19.8 67.5 all-reduce.3
  99.9 34.9 all-gather.3
  148.7 64.8 all-reduce.5
  230.1 34.9 all-gather.5
  279.9 64.9 all-reduce.7
  359.7 34.9 all-gather.7
